TPU v7x, 32 devices: a whole 2x2x4 slice. The times are simulated.
32 devices in a mesh: row: 4 (over y, x), col: 8 (over z, core).
Axes of the slice: x: 2, y: 2, z: 4, core: 2. Of those that a mesh axis runs over, the one named last changes fastest.
Arguments:
- teacher: bfloat16 [16384, 256], replicated, may hold values from -4 to 4
- panel_ids: int32 [2048], P('col'), may hold values from 0 to 16383
- rest_ids: int32 [4, 8, 128], P('row', 'col'), may hold values from 0 to 16383
- inverse: bfloat16 [2048, 2048], replicated, may hold values from -1 to 1, as said below
Outputs:
- trailing: float32 [8, 4, 128, 4, 8, 128], P(None, 'row', None, None, 'col')
- panel_rows: bfloat16 [4, 8, 128, 2048], P('row', 'col')
Inputs may be any that keep to these rules, and one draw needn't show every extreme that they name: `inverse`: zero above the diagonal.
All inputs are finite; a program needn't handle non-finite values.
Results may differ from a plain program's by a relative error of at most 0.0049.
Values may be sent and summed in bfloat16 or wider, within the bound.
A program may use at most 128 MiB of HBM per device.

v0:
```python
import jax
import jax.numpy as jnp
from jax import lax
from jax.sharding import PartitionSpec as P


def gaussian(left_rows, right_rows, inv_scale):
    sq_left = jnp.sum(jnp.square(left_rows.astype(jnp.float32)), axis=-1)
    sq_right = jnp.sum(jnp.square(right_rows.astype(jnp.float32)), axis=-1)
    inner = lax.dot_general(
        left_rows, right_rows, (((1,), (1,)), ((), ())), preferred_element_type=jnp.float32
    )
    return jnp.exp(-inv_scale * (sq_left[:, None] + sq_right[None, :] - 2.0 * inner))


def factor(rows_emb, panel_emb, inverse, inv_scale):
    kernel = gaussian(rows_emb, panel_emb, inv_scale).astype(jnp.bfloat16)
    block_width = inverse.shape[0] // 4
    pieces = []
    for block_at in range(4):
        finish = (block_at + 1) * block_width
        pieces.append(
            lax.dot_general(
                kernel[:, :finish],
                inverse[block_at * block_width : finish, :finish],
                (((1,), (1,)), ((), ())),
                preferred_element_type=jnp.float32,
            )
        )
    return jnp.concatenate(pieces, 1).astype(jnp.bfloat16)


def shards(teacher, panel_ids, rest_ids, inverse):
    n_row = lax.axis_size("row")
    n_col = lax.axis_size("col")
    row_at = lax.axis_index("row")
    col_at = lax.axis_index("col")
    stretch_rows = rest_ids.shape[2]
    inv_scale = 2.0 / teacher.shape[1]
    gathered = lax.all_gather(rest_ids, ("row", "col"), axis=0, tiled=True)
    blocks = gathered.reshape(n_row * n_col, stretch_rows)
    panel = lax.all_gather(panel_ids, "col", axis=0, tiled=True)
    panel_emb = teacher[panel]
    own_ids = lax.dynamic_slice_in_dim(blocks, row_at * n_col + col_at, 1, 0).reshape(stretch_rows)
    col_ids = lax.dynamic_slice_in_dim(
        blocks.reshape(n_row, n_col, stretch_rows), col_at, 1, 1
    ).reshape(-1)
    row_ids = lax.dynamic_slice_in_dim(
        blocks.reshape(n_col, n_row, stretch_rows), row_at, 1, 1
    ).reshape(-1)
    own_factor = factor(teacher[own_ids], panel_emb, inverse, inv_scale)
    col_emb = teacher[col_ids]
    col_factor = lax.all_gather(own_factor, "row", axis=0, tiled=True)
    row_emb = teacher[row_ids]
    kernel = gaussian(row_emb, col_emb, inv_scale)
    row_factor = factor(row_emb, panel_emb, inverse, inv_scale)
    update = lax.dot_general(
        row_factor, col_factor, (((1,), (1,)), ((), ())), preferred_element_type=jnp.float32
    )
    rows_local = jnp.arange(n_col * stretch_rows, dtype=jnp.int32)
    row_index = (
        rows_local // stretch_rows * n_row + row_at
    ) * stretch_rows + rows_local % stretch_rows
    cols_local = jnp.arange(n_row * stretch_rows, dtype=jnp.int32)
    col_index = (
        cols_local // stretch_rows * n_col + col_at
    ) * stretch_rows + cols_local % stretch_rows
    result = kernel - update
    trailing = jnp.where(row_index[:, None] >= col_index[None, :], result, jnp.zeros_like(result))
    return (
        trailing.reshape(n_col, 1, stretch_rows, n_row, 1, stretch_rows),
        own_factor.reshape(1, 1, stretch_rows, own_factor.shape[1]),
    )


def solution(mesh):
    return jax.shard_map(
        shards,
        mesh=mesh,
        in_specs=(P(), P("col"), P("row", "col", None), P()),
        out_specs=(P(None, "row", None, None, "col", None), P("row", "col", None, None)),
        check_vma=False,
    )
```

profile of v0, /device:TPU:0, one launch (start us, length us, event | category | flops | bytes accessed | tf_op | source)
XLA Modules:
  0.0 132.2 jit_solution(9935352924947401463)
XLA Ops:
  7.2 43.5 %all_gather.9 = s32[32,1,128]{2,1,0:T(1,128)S(1)} all-gather(s32[1,1,128]{2,1,0:T(1,128)} %param.6), channel_id=1, replica_groups=mesh['row'=4,'col'=8] {'row','col'}, dimensions={0}, use_global_device_ids=true | all-gather | bytes 16896 | tf_op jit(solution)/shard_map/all_gather | solution.py:40
  50.7 5.2 %gather_fusion.3 = bf16[128,256]{1,0:T(8,128)(2,1)S(1)} fusion(bf16[16384,256]{1,0:T(8,128)(2,1)} %param.4, s32[1024]{0:T(1024)S(1)} %pad_clamp_fusion), kind=kCustom, calls=%fused_computation.3 | custom fusion | bytes 131584 | tf_op jit(solution)/shard_map/gather | solution.py:51
  56.0 9.0 %all-gather = s32[8,1,256]{2,1,0:T(1,128)S(1)} all-gather(s32[1,1,256]{2,1,0:T(1,128)} %bitcast.42), channel_id=1, replica_groups=mesh['row'=4,'col'=8] {'col'}, dimensions={0}, use_global_device_ids=true | all-gather | bytes 9216 | tf_op jit(solution)/shard_map/all_gather | solution.py:42
  65.0 11.1 %gather_fusion.2 = bf16[2048,256]{1,0:T(8,128)(2,1)S(1)} fusion(bf16[16384,256]{1,0:T(8,128)(2,1)} %param.4, s32[2048]{0:T(1024)S(1)} %fusion.46), kind=kCustom, calls=%fused_computation.2 | custom fusion | bytes 2105344 | tf_op jit(solution)/shard_map/gather | solution.py:43
  76.1 0.3 multiply_reduce_fusion
  76.5 0.5 fusion.13
  77.0 1.3 %convolution_convert_fusion.1 = bf16[128,512]{1,0:T(8,128)(2,1)S(1)} fusion(bf16[2048,2048]{1,0:T(8,128)(2,1)} %param.7, bf16[128,2048]{1,0:T(8,128)(2,1)S(1)} %fusion.13), kind=kOutput, calls=%fused_computation.36 | convolution fusion | flops 67174400 | bytes 786432 | tf_op jit(solution)/shard_map/dot_general | solution.py:23
  78.4 1.7 %convolution_convert_fusion.2 = bf16[128,512]{1,0:T(8,128)(2,1)S(1)} fusion(bf16[2048,2048]{1,0:T(8,128)(2,1)} %param.7, bf16[128,2048]{1,0:T(8,128)(2,1)S(1)} %fusion.13), kind=kOutput, calls=%fused_computation.37 | convolution fusion | flops 134283264 | bytes 1441792 | tf_op jit(solution)/shard_map/dot_general | solution.py:23
  80.1 2.4 %fusion.32 = bf16[128,512]{1,0:T(8,128)(2,1)S(1)} fusion(bf16[128,2048]{1,0:T(8,128)(2,1)S(1)} %fusion.13, bf16[2048,2048]{1,0:T(8,128)(2,1)} %param.7), kind=kOutput, calls=%fused_computation.35 | convolution fusion | flops 268500992 | bytes 2752512 | tf_op jit(solution)/shard_map/dot_general | solution.py:23
  82.5 2.1 %fusion.35 = bf16[128,512]{1,0:T(8,128)(2,1)S(1)} fusion(bf16[2048,2048]{1,0:T(8,128)(2,1)} %param.7, bf16[128,2048]{1,0:T(8,128)(2,1)S(1)} %fusion.13), kind=kOutput, calls=%fused_computation.38 | convolution fusion | flops 201392128 | bytes 2097152 | tf_op jit(solution)/shard_map/dot_general | solution.py:23
  84.6 0.8 pad_maximum_fusion
  85.5 7.9 %gather_fusion = bf16[1024,256]{1,0:T(8,128)(2,1)S(1)} fusion(bf16[16384,256]{1,0:T(8,128)(2,1)} %param.4, s32[1024]{0:T(1024)S(1)} %broadcast_clamp_fusion), kind=kCustom, calls=%fused_computation | custom fusion | bytes 1052672 | tf_op jit(solution)/shard_map/gather | solution.py:54
  93.4 6.0 %gather_fusion.1 = bf16[512,256]{1,0:T(8,128)(2,1)S(1)} fusion(bf16[16384,256]{1,0:T(8,128)(2,1)} %param.4, s32[1024]{0:T(1024)S(1)} %pad_clamp_fusion.1), kind=kCustom, calls=%fused_computation.1 | custom fusion | bytes 526336 | tf_op jit(solution)/shard_map/gather | solution.py:52
  99.9 0.8 pad_maximum_fusion.1
  100.7 2.6 %exponential_convert_fusion = bf16[1024,2048]{1,0:T(8,128)(2,1)S(1)} fusion(bf16[1024,256]{1,0:T(8,128)(2,1)S(1)} %gather_fusion, bf16[2048,256]{1,0:T(8,128)(2,1)S(1)} %gather_fusion.2, f32[2048]{0:T(1024)S(1)} %multiply_reduce_fusion, f32[1024]{0:T(1024)S(1)} %multiply_reduce_fusion.1), kind=kOutput, calls=%fused_computation.4 | convolution fusion | flops 1084227584 | bytes 5779456 | tf_op jit(solution)/shard_map/dot_general | solution.py:10
  103.3 0.4 slice-done.1
  103.7 0.7 convolution_convert_fusion
  104.4 1.3 fusion.20
  105.7 2.8 %fusion.23 = bf16[1024,512]{1,0:T(8,128)(2,1)} fusion(bf16[1024,2048]{1,0:T(8,128)(2,1)S(1)} %exponential_convert_fusion, bf16[2048,2048]{1,0:T(8,128)(2,1)S(1)} %bitcast.44), kind=kOutput, calls=%fused_computation.29 | convolution fusion | flops 1611137024 | bytes 5767168 | tf_op jit(solution)/shard_map/dot_general | solution.py:23
  108.5 3.3 %fusion.26 = bf16[1024,512]{1,0:T(8,128)(2,1)} fusion(bf16[1024,2048]{1,0:T(8,128)(2,1)S(1)} %exponential_convert_fusion, bf16[2048,2048]{1,0:T(8,128)(2,1)S(1)} %bitcast.44), kind=kOutput, calls=%fused_computation.31 | convolution fusion | flops 2148007936 | bytes 7340032 | tf_op jit(solution)/shard_map/dot_general | solution.py:23
  111.9 6.3 %all-gather.3.cloned.1.call-done = bf16[512,2048]{1,0:T(8,128)(2,1)} async-done(((bf16[128,2048]{1,0:T(8,128)(2,1)}), bf16[512,2048]{1,0:T(8,128)(2,1)}) %all-gather.3.cloned.1.call-update) | async-done | bytes 2097168 | tf_op jit(solution)/shard_map/all_gather | solution.py:53
  118.2 4.5 %fusion = f32[1024,512]{1,0:T(8,128)S(1)} fusion(bf16[512,2048]{1,0:T(8,128)(2,1)} %all-gather.3.cloned.1.call-done, bf16[1024,512]{1,0:T(8,128)(2,1)} %fusion.26, bf16[1024,512]{1,0:T(8,128)(2,1)} %fusion.23, bf16[1024,512]{1,0:T(8,128)(2,1)S(1)} %fusion.20, bf16[1024,512]{1,0:T(8,128)(2,1)S(1)} %convolution_convert_fusion), kind=kOutput, calls=%fused_computation.5 | convolution fusion | flops 2164260864 | bytes 8388608 | tf_op jit(solution)/shard_map/dot_general | solution.py:57
  122.8 0.8 subtract_select_fusion
  123.6 1.7 %reshape.218 = f32[8,1,128,4,1,128]{5,3,2,0,4,1:T(4,128)} reshape(f32[1024,512]{1,0:T(8,128)S(1)} %subtract_select_fusion) | data formatting | bytes 4194304 | tf_op jit(solution)/shard_map/reshape | solution.py:71
  (18 shorter events, 0.6 us)
Async XLA Ops:
  7.2 111.1 %all-gather.3.cloned.1.call-start = ((), (), s32[]{:S(2)}) async-start(), calls=%async_computation | async-start | bytes 2621440 | tf_op jit(solution)/shard_map/all_gather | solution.py:53
  99.9 3.4 %slice-start = ((s8[8388608]{0:T(1024)(128)(4,1)}), s8[4194304]{0:T(1024)(128)(4,1)S(1)}, s32[]{:S(2)}) async-start(s8[8388608]{0:T(1024)(128)(4,1)} %bitcast.43), calls=%async_computation.1 | async-start | bytes 8388608
  100.7 3.0 %slice-start.1 = ((s8[8388608]{0:T(1024)(128)(4,1)}), s8[4194304]{0:T(1024)(128)(4,1)S(1)}, s32[]{:S(2)}) async-start(s8[8388608]{0:T(1024)(128)(4,1)} %bitcast.43), calls=%async_computation.2 | async-start | bytes 8388608
Sparse Core Ops, SparseCore 0:
  85.6 32.6 all-gather.2
where the time goes:
time: 133 us; the launch traced here: 132 us
  blocking collectives  52.5 us (39%)
  local copies, waits for them, and re-layouts  32.4 us (24%)
  matrix products  24.1 us (18%)
  between operations  14.2 us (11%)
  waiting for transfers between devices  6.36 us (5%)
  other arithmetic  2.57 us (2%)
    all_gather x1, blocking collectives, shards(): gathered = lax.all_gather(rest_ids, ('row', 'col'), axis=0, tiled=True)  43.5 us
    dot_general x8, matrix products, factor(): lax.dot_general(kernel[:, :finish], inverse[block_at * block_width:finish...  15.7 us
    gather x1, local copies, waits for them, and re-layouts, shards(): panel_emb = teacher[panel]  11.1 us
    all_gather x1, blocking collectives, shards(): panel = lax.all_gather(panel_ids, 'col', axis=0, tiled=True)  8.99 us
    gather x1, local copies, waits for them, and re-layouts, shards(): row_emb = teacher[row_ids]  7.92 us
    all_gather x1, waiting for transfers between devices, shards(): col_factor = lax.all_gather(own_factor, 'row', axis=0, tiled=True)  6.34 us
    gather x1, local copies, waits for them, and re-layouts, shards(): col_emb = teacher[col_ids]  6.02 us
    gather x1, local copies, waits for them, and re-layouts, shards(): own_factor = factor(teacher[own_ids], panel_emb, inverse, inv_scale)  5.22 us
  transfers between devices with their start and end apart: 1, of which 1 were waited for; matrix products, arithmetic and copies ran while one was open for 20% of the time, Pallas kernels for 0%

commit v1 on v0

v1 whole, which is shorter than its diff:
```python
import functools

import jax
import jax.numpy as jnp
from jax import lax
from jax.experimental import pallas as pl
from jax.experimental.pallas import tpu as pltpu
from jax.sharding import PartitionSpec as P

MESH = pl.DeviceIdType.MESH


def exchange_kernel(n_row, n_col, rest_ref, panel_ref, panel_out, row_out, col_out, send_sem, row_sem, col_sem, panel_sem):
    row_at = lax.axis_index("row")
    col_at = lax.axis_index("col")
    me = row_at * n_col + col_at
    barrier = pltpu.get_barrier_semaphore()
    count = n_row * n_col

    def greet(step, carry):
        other = lax.rem(me + step, count)
        pl.semaphore_signal(
            barrier, inc=1, device_id=(other // n_col, lax.rem(other, n_col)), device_id_type=MESH
        )
        return carry

    lax.fori_loop(1, count, greet, 0)
    panel_out[col_at] = panel_ref[0]
    col_out[row_at] = rest_ref[0]
    row_role = lax.rem(me, n_row)
    place = me // n_row

    @pl.when(row_role == row_at)
    def _():
        row_out[place] = rest_ref[0]

    pl.semaphore_wait(barrier, count - 1)

    def panel_copy(slot, target):
        return pltpu.make_async_remote_copy(
            src_ref=panel_ref.at[0], dst_ref=panel_out.at[slot],
            send_sem=send_sem.at[target], recv_sem=panel_sem.at[slot],
            device_id=(row_at, target), device_id_type=MESH,
        )

    def row_copy(slot, target):
        return pltpu.make_async_remote_copy(
            src_ref=rest_ref.at[0], dst_ref=row_out.at[slot],
            send_sem=send_sem.at[n_col + target], recv_sem=row_sem.at[slot],
            device_id=(row_role, target), device_id_type=MESH,
        )

    def col_copy(slot, target):
        return pltpu.make_async_remote_copy(
            src_ref=rest_ref.at[0], dst_ref=col_out.at[slot],
            send_sem=send_sem.at[2 * n_col + target], recv_sem=col_sem.at[slot],
            device_id=(target, col_at), device_id_type=MESH,
        )

    def each(length, skip, act):
        for at in range(length):
            pl.when(jnp.logical_not(skip(at)))(functools.partial(act, at))

    to_self = lambda at: jnp.logical_and(row_role == row_at, at == col_at)
    from_self = lambda at: at * n_row + row_at == me
    each(n_col, lambda at: at == col_at, lambda at: panel_copy(col_at, at).start())
    each(n_col, to_self, lambda at: row_copy(place, at).start())
    each(n_row, lambda at: at == row_at, lambda at: col_copy(row_at, at).start())
    each(n_col, lambda at: at == col_at, lambda at: panel_copy(at, at).wait_recv())
    each(n_col, from_self, lambda at: row_copy(at, at).wait_recv())
    each(n_row, lambda at: at == row_at, lambda at: col_copy(at, at).wait_recv())
    each(n_col, lambda at: at == col_at, lambda at: panel_copy(col_at, at).wait_send())
    each(n_col, to_self, lambda at: row_copy(place, at).wait_send())
    each(n_row, lambda at: at == row_at, lambda at: col_copy(row_at, at).wait_send())


def exchange(rest_ids, panel_ids, n_row, n_col):
    stretch = rest_ids.shape[2]
    width = panel_ids.shape[0]
    vmem = pl.BlockSpec(memory_space=pltpu.VMEM)
    return pl.pallas_call(
        functools.partial(exchange_kernel, n_row, n_col),
        out_shape=(
            jax.ShapeDtypeStruct((n_col, 1, width), jnp.int32),
            jax.ShapeDtypeStruct((n_col, 1, stretch), jnp.int32),
            jax.ShapeDtypeStruct((n_row, 1, stretch), jnp.int32),
        ),
        in_specs=[vmem] * 2,
        out_specs=(vmem,) * 3,
        scratch_shapes=[
            pltpu.SemaphoreType.DMA((2 * n_col + n_row,)),
            pltpu.SemaphoreType.DMA((n_col,)),
            pltpu.SemaphoreType.DMA((n_row,)),
            pltpu.SemaphoreType.DMA((n_col,)),
        ],
        compiler_params=pltpu.CompilerParams(collective_id=0, has_side_effects=True),
        name="exchange",
    )(rest_ids, panel_ids.reshape(1, 1, width))


def nt_dot(left, right):
    return lax.dot_general(left, right, (((1,), (1,)), ((), ())), preferred_element_type=jnp.float32)


def gram_kernel(n_row, n_col, stretch, emb_ref, inv_hbm, trail_ref, own_ref, inv_ref, cross_ref, fac_ref, norm_ref, inv_sem):
    width = inv_hbm.shape[0]
    block = 256
    blocks = width // block
    total = emb_ref.shape[0] - width
    n_rows = n_col * stretch
    unit = 2.0 / emb_ref.shape[1] * 1.4426950408889634
    row_at = lax.axis_index("row")
    col_at = lax.axis_index("col")

    def load(at):
        rows, cols = pl.ds(at * block, block), pl.ds(0, (at + 1) * block)
        return pltpu.make_async_copy(inv_hbm.at[rows, cols], inv_ref.at[rows, cols], inv_sem.at[at])

    for at in range(blocks):
        load(at).start()

    def across(value):
        square = jnp.square(value.astype(jnp.float32))
        high = square.astype(jnp.bfloat16)
        low = (square - high.astype(jnp.float32)).astype(jnp.bfloat16)
        ones = jnp.ones((8, value.shape[1]), jnp.bfloat16)
        return (nt_dot(ones, high) + nt_dot(ones, low)) * unit

    def down(value):
        return jnp.sum(jnp.square(value.astype(jnp.float32)), axis=-1, keepdims=True) * unit

    for at in range(blocks):
        norm_ref[:, at * block : (at + 1) * block] = across(emb_ref[at * block : (at + 1) * block, :])

    def gram(left, left_norm, right, right_norm):
        return jnp.exp2(nt_dot(left, right) * (2.0 * unit) - (left_norm + right_norm))

    tile = 512

    def factor_tile(start, first):
        rows = pl.ds(start, tile)
        left = emb_ref[pl.ds(width + start, tile), :]
        left_norm = down(left)
        for at in range(blocks):
            cols = slice(at * block, (at + 1) * block)
            cross_ref[:, cols] = gram(left, left_norm, emb_ref[cols, :], norm_ref[0:1, cols]).astype(jnp.bfloat16)
            if first:
                load(at).wait()
            fac_ref[rows, cols] = nt_dot(
                cross_ref[:, : (at + 1) * block], inv_ref[cols, : (at + 1) * block]
            ).astype(jnp.bfloat16)

    factor_tile(n_rows, True)
    for start in range(n_rows + tile, total, tile):
        factor_tile(start, False)
    own_ref[...] = fac_ref[pl.ds(pl.multiple_of(n_rows + row_at * stretch, stretch), stretch), :]

    ahead = lax.broadcasted_iota(jnp.int32, (stretch, stretch), 0) - lax.broadcasted_iota(
        jnp.int32, (stretch, stretch), 1
    )
    pair = 2 if n_row % 2 == 0 else 1
    for start in range(0, n_rows, tile):
        factor_tile(start, False)
        left = emb_ref[pl.ds(width + start, tile), :]
        left_norm = down(left)
        last = (start + tile) // stretch - 1
        for low in range(0, n_row, pair):
            if last * n_row + n_row - 1 >= low * n_col:
                first_col = n_rows + low * stretch
                span = pl.ds(first_col, pair * stretch)
                right = emb_ref[pl.ds(width + first_col, pair * stretch), :]
                value = gram(left, left_norm, right, across(right)[0:1]) - nt_dot(
                    fac_ref[pl.ds(start, tile), :], fac_ref[span, :]
                )
            else:
                value = None
            for q in range(start // stretch, last + 1):
                for p in range(low, low + pair):
                    place = pl.ds(q * stretch * n_row + p, stretch, stride=n_row)
                    if q * n_row + n_row - 1 < p * n_col:
                        trail_ref[place, :] = jnp.zeros((stretch, stretch), jnp.float32)
                    else:
                        top = q * stretch - start
                        side = (p - low) * stretch
                        part = value[top : top + stretch, side : side + stretch]
                        gap = (p * n_col + col_at - q * n_row - row_at) * stretch
                        trail_ref[place, :] = jnp.where(ahead >= gap, part, 0.0)


def shards(teacher, panel_ids, rest_ids, inverse):
    n_row = lax.axis_size("row")
    n_col = lax.axis_size("col")
    stretch = rest_ids.shape[2]
    width = inverse.shape[0]
    panel, row_ids, col_ids = exchange(rest_ids, panel_ids, n_row, n_col)
    ids = jnp.concatenate([panel.reshape(-1), row_ids.reshape(-1), col_ids.reshape(-1)])
    emb = teacher.at[ids].get(mode="promise_in_bounds")
    total = emb.shape[0] - width
    vmem = pl.BlockSpec(memory_space=pltpu.VMEM)
    trailing, own_factor = pl.pallas_call(
        functools.partial(gram_kernel, n_row, n_col, stretch),
        out_shape=(
            jax.ShapeDtypeStruct((n_col * stretch * n_row, stretch), jnp.float32),
            jax.ShapeDtypeStruct((stretch, width), jnp.bfloat16),
        ),
        in_specs=[vmem, pl.BlockSpec(memory_space=pltpu.HBM)],
        out_specs=(vmem, vmem),
        scratch_shapes=[
            pltpu.VMEM((width, width), jnp.bfloat16),
            pltpu.VMEM((512, width), jnp.bfloat16),
            pltpu.VMEM((total, width), jnp.bfloat16),
            pltpu.VMEM((8, width), jnp.float32),
            pltpu.SemaphoreType.DMA((width // 256,)),
        ],
        compiler_params=pltpu.CompilerParams(vmem_limit_bytes=56 * 1024 * 1024),
        name="gram",
    )(emb, inverse)
    return (
        trailing.reshape(n_col, 1, stretch, n_row, 1, stretch),
        own_factor.reshape(1, 1, stretch, width),
    )


def solution(mesh):
    return jax.shard_map(
        shards,
        mesh=mesh,
        in_specs=(P(), P("col"), P("row", "col", None), P()),
        out_specs=(P(None, "row", None, None, "col", None), P("row", "col", None, None)),
        check_vma=False,
    )
```

time: 133 us -> 44.8 us (0.34)
  blocking collectives: 52.5 us -> 0 us
  Pallas kernels: 0 us -> 29.6 us
  matrix products: 24.1 us -> 0 us
  local copies, waits for them, and re-layouts: 32.4 us -> 13.5 us
  between operations: 14.2 us -> 0.65 us
  waiting for transfers between devices: 6.36 us -> 0 us
  other arithmetic: 2.57 us -> 0.76 us
    all_gather x2 -> x0, blocking collectives: 52.5 us -> none  [the longest x1 43.5 us: shards(): gathered = lax.all_gather(rest_ids, ('row', 'col'), axis=0, tiled=True)]
    pallas_call x0 -> x2, Pallas kernels: none -> 29.6 us  [the longest x1 18.5 us: shards(): pl.pallas_call(functools.partial(gram_kernel, n_row, n_col, stretch), out...]
    dot_general x12 -> x0, matrix products: 24.1 us -> none  [the longest x8 15.7 us: factor(): lax.dot_general(kernel[:, :finish], inverse[block_at * block_width:finish...]
    gather x4 -> x1, local copies, waits for them, and re-layouts: 30.3 us -> 13.5 us  [shards(): emb = teacher.at[ids].get(mode='promise_in_bounds')]
    all_gather x1 -> x0, waiting for transfers between devices: 6.34 us -> none  [shards(): col_factor = lax.all_gather(own_factor, 'row', axis=0, tiled=True)]
    reshape x1 -> x0, local copies, waits for them, and re-layouts: 1.72 us -> none  [shards(): trailing.reshape(n_col, 1, stretch_rows, n_row, 1, stretch_rows)]
    concatenate x2 -> x0, other arithmetic: 1.69 us -> none  [factor(): return jnp.concatenate(pieces, 1).astype(jnp.bfloat16)]
  transfers between devices with their start and end apart: 1 -> 0, of which waited for: 1 -> 0; matrix products, arithmetic and copies ran while one was open for 20% -> 0% of each run, Pallas kernels for 0% -> 0%
where the time goes in v1:
time: 44.8 us; the launch traced here: 44.5 us
  Pallas kernels  29.6 us (66%)
  local copies, waits for them, and re-layouts  13.5 us (30%)
  other arithmetic  0.76 us (2%)
  between operations  0.65 us (1%)
    pallas_call x1, Pallas kernels, shards(): pl.pallas_call(functools.partial(gram_kernel, n_row, n_col, stretch), out...  18.5 us
    gather x1, local copies, waits for them, and re-layouts, shards(): emb = teacher.at[ids].get(mode='promise_in_bounds')  13.5 us
    pallas_call x1, Pallas kernels, exchange(): pl.pallas_call(functools.partial(exchange_kernel, n_row, n_col), out_shap...  11.1 us

profile of v1, /device:TPU:0, one launch (start us, length us, event | category | flops | bytes accessed | tf_op | source)
XLA Modules:
  0.0 44.5 jit_solution(12610211079616923931)
XLA Ops:
  0.6 11.1 %exchange.1 = (s32[8,1,256]{2,1,0:T(1,128)}, s32[8,1,128]{2,1,0:T(1,128)}, s32[4,1,128]{2,1,0:T(1,128)}) custom-call(s32[1,1,128]{2,1,0:T(1,128)} %rest_ref.1, s32[1,1,256]{2,1,0:T(1,128)} %bitcast.13), custom_call_target="tpu_custom_call" | custom-call | tf_op jit(solution)/shard_map/exchange/pallas_call | solution.py:81
  11.7 0.8 %fusion = s32[3584]{0:T(1024)S(1)} fusion(s32[512,1]{0,1:T(1,128)} %bitcast.10, s32[1024,1]{0,1:T(1,128)} %bitcast.9, s32[2048,1]{0,1:T(1,128)} %bitcast.8), kind=kLoop, calls=%fused_computation.3 | loop fusion | flops 17920 | bytes 28672 | tf_op jit(solution)/shard_map/select_n | solution.py:197
  12.5 13.5 %gather_fusion = bf16[3584,256]{1,0:T(8,128)(2,1)} fusion(bf16[16384,256]{1,0:T(8,128)(2,1)} %param.4, s32[4096]{0:T(1024)S(1)} %pad_clamp_fusion), kind=kCustom, calls=%fused_computation | custom fusion | bytes 3684352 | tf_op jit(solution)/shard_map/gather | solution.py:197
  26.1 18.5 %gram.1 = (f32[4096,128]{1,0:T(8,128)}, bf16[128,2048]{1,0:T(8,128)(2,1)}) custom-call(bf16[3584,256]{1,0:T(8,128)(2,1)} %gather_fusion, bf16[2048,2048]{1,0:T(8,128)(2,1)} %inv_hbm.1), custom_call_target="tpu_custom_call" | custom-call | tf_op jit(solution)/shard_map/gram/pallas_call | solution.py:200
  (1 shorter events, 0.0 us)

commit v2 on v1

--- a/solution.py
+++ b/solution.py
@@ -10,7 +10,20 @@
 MESH = pl.DeviceIdType.MESH
 
 
-def exchange_kernel(n_row, n_col, rest_ref, panel_ref, panel_out, row_out, col_out, send_sem, row_sem, col_sem, panel_sem):
+def exchange_kernel(
+    n_row, n_col, rest_ref, panel_ref, table_hbm, emb_ref,
+    panel_out, row_out, col_out, panel_ids, row_ids, col_ids, landed, table, picked,
+    send_sem, row_sem, col_sem, panel_sem, table_sem, ids_sem,
+):
+    pieces = table_sem.shape[0]
+    piece = table_hbm.shape[0] // pieces
+
+    def load(at):
+        rows = pl.ds(at * piece, piece)
+        return pltpu.make_async_copy(table_hbm.at[rows], landed.at[rows], table_sem.at[at])
+
+    for at in range(pieces):
+        load(at).start()
     row_at = lax.axis_index("row")
     col_at = lax.axis_index("col")
     me = row_at * n_col + col_at
@@ -66,36 +79,80 @@
     each(n_col, lambda at: at == col_at, lambda at: panel_copy(col_at, at).start())
     each(n_col, to_self, lambda at: row_copy(place, at).start())
     each(n_row, lambda at: at == row_at, lambda at: col_copy(row_at, at).start())
+    for at in range(pieces):
+        load(at).wait()
+
+        def widen(step, carry, at=at):
+            rows = pl.ds(pl.multiple_of(at * piece + step * 64, 64), 64)
+            table[rows, :] = landed[rows, :].astype(jnp.float32)
+            return carry
+
+        lax.fori_loop(0, piece // 64, widen, 0)
     each(n_col, lambda at: at == col_at, lambda at: panel_copy(at, at).wait_recv())
     each(n_col, from_self, lambda at: row_copy(at, at).wait_recv())
     each(n_row, lambda at: at == row_at, lambda at: col_copy(at, at).wait_recv())
     each(n_col, lambda at: at == col_at, lambda at: panel_copy(col_at, at).wait_send())
     each(n_col, to_self, lambda at: row_copy(place, at).wait_send())
     each(n_row, lambda at: at == row_at, lambda at: col_copy(row_at, at).wait_send())
-
-
-def exchange(rest_ids, panel_ids, n_row, n_col):
+    groups = ((panel_out, panel_ids), (row_out, row_ids), (col_out, col_ids))
+    moves = [pltpu.make_async_copy(src, dst, ids_sem.at[at]) for at, (src, dst) in enumerate(groups)]
+    for move in moves:
+        move.start()
+    for move in moves:
+        move.wait()
+    unroll = 16
+    first = 0
+    for _, ids in groups:
+        count, _, span = ids.shape
+
+        def pick(step, carry, ids=ids, span=span, first=first):
+            at = step * unroll
+            block, inner = at // span, lax.rem(at, span)
+            for lane in range(unroll):
+                row = ids[block, 0, inner + lane]
+                picked[pl.ds(pl.multiple_of(first + at, unroll) + lane, 1), :] = table[pl.ds(row, 1), :]
+            return carry
+
+        lax.fori_loop(0, count * span // unroll, pick, 0)
+        first += count * span
+
+    def narrow(step, carry):
+        rows = pl.ds(pl.multiple_of(step * 64, 64), 64)
+        emb_ref[rows, :] = picked[rows, :].astype(jnp.bfloat16)
+        return carry
+
+    lax.fori_loop(0, first // 64, narrow, 0)
+
+
+def exchange(rest_ids, panel_ids, teacher, n_row, n_col):
     stretch = rest_ids.shape[2]
     width = panel_ids.shape[0]
+    total = n_col * width + (n_col + n_row) * stretch
+    shapes = ((n_col, 1, width), (n_col, 1, stretch), (n_row, 1, stretch))
     vmem = pl.BlockSpec(memory_space=pltpu.VMEM)
     return pl.pallas_call(
         functools.partial(exchange_kernel, n_row, n_col),
-        out_shape=(
-            jax.ShapeDtypeStruct((n_col, 1, width), jnp.int32),
-            jax.ShapeDtypeStruct((n_col, 1, stretch), jnp.int32),
-            jax.ShapeDtypeStruct((n_row, 1, stretch), jnp.int32),
-        ),
-        in_specs=[vmem] * 2,
-        out_specs=(vmem,) * 3,
-        scratch_shapes=[
+        out_shape=jax.ShapeDtypeStruct((total, teacher.shape[1]), teacher.dtype),
+        in_specs=[vmem, vmem, pl.BlockSpec(memory_space=pltpu.HBM)],
+        out_specs=vmem,
+        scratch_shapes=[pltpu.VMEM(shape, jnp.int32) for shape in shapes]
+        + [pltpu.SMEM(shape, jnp.int32) for shape in shapes]
+        + [
+            pltpu.VMEM(teacher.shape, teacher.dtype),
+            pltpu.VMEM(teacher.shape, jnp.float32),
+            pltpu.VMEM((total, teacher.shape[1]), jnp.float32),
             pltpu.SemaphoreType.DMA((2 * n_col + n_row,)),
             pltpu.SemaphoreType.DMA((n_col,)),
             pltpu.SemaphoreType.DMA((n_row,)),
             pltpu.SemaphoreType.DMA((n_col,)),
+            pltpu.SemaphoreType.DMA((8,)),
+            pltpu.SemaphoreType.DMA((3,)),
         ],
-        compiler_params=pltpu.CompilerParams(collective_id=0, has_side_effects=True),
+        compiler_params=pltpu.CompilerParams(
+            collective_id=0, has_side_effects=True, vmem_limit_bytes=52 * 1024 * 1024
+        ),
         name="exchange",
-    )(rest_ids, panel_ids.reshape(1, 1, width))
+    )(rest_ids, panel_ids.reshape(1, 1, width), teacher)
 
 
 def nt_dot(left, right):
@@ -192,9 +249,7 @@
     n_col = lax.axis_size("col")
     stretch = rest_ids.shape[2]
     width = inverse.shape[0]
-    panel, row_ids, col_ids = exchange(rest_ids, panel_ids, n_row, n_col)
-    ids = jnp.concatenate([panel.reshape(-1), row_ids.reshape(-1), col_ids.reshape(-1)])
-    emb = teacher.at[ids].get(mode="promise_in_bounds")
+    emb = exchange(rest_ids, panel_ids, teacher, n_row, n_col)
     total = emb.shape[0] - width
     vmem = pl.BlockSpec(memory_space=pltpu.VMEM)
     trailing, own_factor = pl.pallas_call(
@@ -212,7 +267,7 @@
             pltpu.VMEM((8, width), jnp.float32),
             pltpu.SemaphoreType.DMA((width // 256,)),
         ],
-        compiler_params=pltpu.CompilerParams(vmem_limit_bytes=56 * 1024 * 1024),
+        compiler_params=pltpu.CompilerParams(vmem_limit_bytes=50 * 1024 * 1024),
         name="gram",
     )(emb, inverse)
     return (

time: 44.8 us -> 49 us (1.094)
  Pallas kernels: 29.6 us -> 46.9 us
  local copies, waits for them, and re-layouts: 13.5 us -> 1.33 us
  other arithmetic: 0.76 us -> 0 us
    pallas_call x1, Pallas kernels: 11.1 us -> 29.8 us  [exchange(): pl.pallas_call(functools.partial(exchange_kernel, n_row, n_col), out_shap...]
    gather x1 -> x0, local copies, waits for them, and re-layouts: 13.5 us -> none  [shards(): emb = teacher.at[ids].get(mode='promise_in_bounds')]
    pallas_call x1, Pallas kernels: 18.5 us -> 17.1 us  [shards(): pl.pallas_call(functools.partial(gram_kernel, n_row, n_col, stretch), out...]
    unnamed x0 -> x4, local copies, waits for them, and re-layouts: none -> 1.33 us
    select_n x1 -> x0, other arithmetic: 0.76 us -> none  [shards(): emb = teacher.at[ids].get(mode='promise_in_bounds')]
where the time goes in v2:
time: 49 us; the launch traced here: 48.9 us
  Pallas kernels  46.9 us (96%)
  local copies, waits for them, and re-layouts  1.33 us (3%)
  between operations  0.65 us (1%)
    pallas_call x1, Pallas kernels, exchange(): pl.pallas_call(functools.partial(exchange_kernel, n_row, n_col), out_shap...  29.8 us
    pallas_call x1, Pallas kernels, shards(): pl.pallas_call(functools.partial(gram_kernel, n_row, n_col, stretch), out...  17.1 us
    unnamed x4, local copies, waits for them, and re-layouts  1.33 us

profile of v2, /device:TPU:0, one launch (start us, length us, event | category | flops | bytes accessed | tf_op | source)
XLA Modules:
  0.0 48.9 jit_solution(4740503034610252296)
XLA Ops:
  0.6 0.0 copy-start
  0.6 0.7 %copy-done = s32[256]{0:T(256)S(1)} copy-done((s32[256]{0:T(256)S(1)}, s32[256]{0:T(256)}, u32[]{:S(2)}) %copy-start) | copy-done | bytes 1048
  1.3 0.0 copy-start.1
  1.3 0.7 %copy-done.1 = s32[1,1,128]{2,1,0:T(1,128)S(1)} copy-done((s32[1,1,128]{2,1,0:T(1,128)S(1)}, s32[1,1,128]{2,1,0:T(1,128)}, u32[]{:S(2)}) %copy-start.1) | copy-done | bytes 536
  2.0 29.8 %exchange.1.emb_ref = bf16[3584,256]{1,0:T(8,128)(2,1)S(1)} custom-call(s32[1,1,128]{2,1,0:T(1,128)S(1)} %copy-done.1, s32[1,1,256]{2,1,0:T(1,128)S(1)} %bitcast.5, bf16[16384,256]{1,0:T(8,128)(2,1)} %table_hbm.1), custom_call_target="tpu_custom_call" | custom-call | tf_op jit(solution)/shard_map/exchange/pallas_call | solution.py:133
  31.8 17.1 %gram.1 = (f32[4096,128]{1,0:T(8,128)}, bf16[128,2048]{1,0:T(8,128)(2,1)}) custom-call(bf16[3584,256]{1,0:T(8,128)(2,1)S(1)} %exchange.1.emb_ref, bf16[2048,2048]{1,0:T(8,128)(2,1)} %inv_hbm.1), custom_call_target="tpu_custom_call" | custom-call | tf_op jit(solution)/shard_map/gram/pallas_call | solution.py:255
Async XLA Ops:
  0.6 0.7 %copy-start = (s32[256]{0:T(256)S(1)}, s32[256]{0:T(256)}, u32[]{:S(2)}) copy-start(s32[256]{0:T(256)} %param.5) | copy-start | bytes 3076
  1.3 0.7 %copy-start.1 = (s32[1,1,128]{2,1,0:T(1,128)S(1)}, s32[1,1,128]{2,1,0:T(1,128)}, u32[]{:S(2)}) copy-start(s32[1,1,128]{2,1,0:T(1,128)} %rest_ref.1) | copy-start | bytes 1540

commit v3 on v2

--- a/solution.py
+++ b/solution.py
@@ -16,6 +16,8 @@
     send_sem, row_sem, col_sem, panel_sem, table_sem, ids_sem,
 ):
     pieces = table_sem.shape[0]
+    lanes = table.shape[1]
+    halves = table_hbm.shape[1] // lanes
     piece = table_hbm.shape[0] // pieces
 
     def load(at):
@@ -84,7 +86,10 @@
 
         def widen(step, carry, at=at):
             rows = pl.ds(pl.multiple_of(at * piece + step * 64, 64), 64)
-            table[rows, :] = landed[rows, :].astype(jnp.float32)
+            wide = landed[rows, :].astype(jnp.float32)
+            for half in range(halves):
+                place = pl.ds((at * piece + step * 64) * halves + half, 64, stride=halves)
+                table[place, :] = wide[:, half * lanes : (half + 1) * lanes]
             return carry
 
         lax.fori_loop(0, piece // 64, widen, 0)
@@ -100,25 +105,26 @@
         move.start()
     for move in moves:
         move.wait()
-    unroll = 16
     first = 0
     for _, ids in groups:
         count, _, span = ids.shape
 
-        def pick(step, carry, ids=ids, span=span, first=first):
-            at = step * unroll
-            block, inner = at // span, lax.rem(at, span)
-            for lane in range(unroll):
-                row = ids[block, 0, inner + lane]
-                picked[pl.ds(pl.multiple_of(first + at, unroll) + lane, 1), :] = table[pl.ds(row, 1), :]
+        def pick(block, carry, ids=ids, span=span, first=first):
+            start = pl.multiple_of((first + block * span) * halves, span * halves)
+            home = picked.at[pl.ds(start, span * halves)]
+            for lane in range(span):
+                row = ids[block, 0, lane] * halves
+                home[lane * halves : (lane + 1) * halves, :] = table[pl.ds(row, halves), :]
             return carry
 
-        lax.fori_loop(0, count * span // unroll, pick, 0)
+        lax.fori_loop(0, count, pick, 0)
         first += count * span
 
     def narrow(step, carry):
         rows = pl.ds(pl.multiple_of(step * 64, 64), 64)
-        emb_ref[rows, :] = picked[rows, :].astype(jnp.bfloat16)
+        for half in range(halves):
+            value = picked[pl.ds(step * 64 * halves + half, 64, stride=halves), :]
+            emb_ref[rows, half * lanes : (half + 1) * lanes] = value.astype(jnp.bfloat16)
         return carry
 
     lax.fori_loop(0, first // 64, narrow, 0)
@@ -139,8 +145,8 @@
         + [pltpu.SMEM(shape, jnp.int32) for shape in shapes]
         + [
             pltpu.VMEM(teacher.shape, teacher.dtype),
-            pltpu.VMEM(teacher.shape, jnp.float32),
-            pltpu.VMEM((total, teacher.shape[1]), jnp.float32),
+            pltpu.VMEM((teacher.size // 128, 128), jnp.float32),
+            pltpu.VMEM((total * teacher.shape[1] // 128, 128), jnp.float32),
             pltpu.SemaphoreType.DMA((2 * n_col + n_row,)),
             pltpu.SemaphoreType.DMA((n_col,)),
             pltpu.SemaphoreType.DMA((n_row,)),

time: 49 us -> 34.5 us (0.70)
  Pallas kernels: 46.9 us -> 32.4 us
    pallas_call x1, Pallas kernels: 29.8 us -> 15.3 us  [exchange(): pl.pallas_call(functools.partial(exchange_kernel, n_row, n_col), out_shap...]
where the time goes in v3:
time: 34.5 us; the launch traced here: 34.4 us
  Pallas kernels  32.4 us (94%)
  local copies, waits for them, and re-layouts  1.33 us (4%)
  between operations  0.65 us (2%)
    pallas_call x1, Pallas kernels, shards(): pl.pallas_call(functools.partial(gram_kernel, n_row, n_col, stretch), out...  17.1 us
    pallas_call x1, Pallas kernels, exchange(): pl.pallas_call(functools.partial(exchange_kernel, n_row, n_col), out_shap...  15.3 us
    unnamed x4, local copies, waits for them, and re-layouts  1.33 us

profile of v3, /device:TPU:0, one launch (start us, length us, event | category | flops | bytes accessed | tf_op | source)
XLA Modules:
  0.0 34.4 jit_solution(17586242803317331084)
XLA Ops:
  0.6 0.0 copy-start
  0.6 0.7 %copy-done = s32[256]{0:T(256)S(1)} copy-done((s32[256]{0:T(256)S(1)}, s32[256]{0:T(256)}, u32[]{:S(2)}) %copy-start) | copy-done | bytes 1048
  1.3 0.0 copy-start.1
  1.3 0.7 %copy-done.1 = s32[1,1,128]{2,1,0:T(1,128)S(1)} copy-done((s32[1,1,128]{2,1,0:T(1,128)S(1)}, s32[1,1,128]{2,1,0:T(1,128)}, u32[]{:S(2)}) %copy-start.1) | copy-done | bytes 536
  2.0 15.3 %exchange.1.emb_ref = bf16[3584,256]{1,0:T(8,128)(2,1)S(1)} custom-call(s32[1,1,128]{2,1,0:T(1,128)S(1)} %copy-done.1, s32[1,1,256]{2,1,0:T(1,128)S(1)} %bitcast.5, bf16[16384,256]{1,0:T(8,128)(2,1)} %table_hbm.1), custom_call_target="tpu_custom_call" | custom-call | tf_op jit(solution)/shard_map/exchange/pallas_call | solution.py:139
  17.3 17.1 %gram.1 = (f32[4096,128]{1,0:T(8,128)}, bf16[128,2048]{1,0:T(8,128)(2,1)}) custom-call(bf16[3584,256]{1,0:T(8,128)(2,1)S(1)} %exchange.1.emb_ref, bf16[2048,2048]{1,0:T(8,128)(2,1)} %inv_hbm.1), custom_call_target="tpu_custom_call" | custom-call | tf_op jit(solution)/shard_map/gram/pallas_call | solution.py:261
Async XLA Ops:
  0.6 0.7 %copy-start = (s32[256]{0:T(256)S(1)}, s32[256]{0:T(256)}, u32[]{:S(2)}) copy-start(s32[256]{0:T(256)} %param.5) | copy-start | bytes 3076
  1.3 0.7 %copy-start.1 = (s32[1,1,128]{2,1,0:T(1,128)S(1)}, s32[1,1,128]{2,1,0:T(1,128)}, u32[]{:S(2)}) copy-start(s32[1,1,128]{2,1,0:T(1,128)} %rest_ref.1) | copy-start | bytes 1540
